TPU v7x, 256 devices: a whole 4x4x8 slice. The times are simulated.
256 devices in a mesh: seg: 4 (over y), bond: 64 (over z, x, core).
Axes of the slice: x: 4, y: 4, z: 8, core: 2. Of those that a mesh axis runs over, the one named last changes fastest.
Arguments:
- sites: float32 [4, 2, 8192, 8192], P('seg', None, 'bond'), may hold values from -0.6629126 to 0.6629126, as said below
- boundary: float32 [8192], P('bond'), may hold values from -6 to 6
- bits: int32 [32, 4], P(None, 'seg'), may hold values from 0 to 1
- order: int32 [32], replicated, may hold values from 0 to 31, each once
Outputs:
- probs: float32 [32, 4], P(None, 'seg')
Inputs may be any that keep to these rules, and one draw needn't show every extreme that they name: `order`: each slot number appears once. `sites`: real entries.
All inputs are finite; a program needn't handle non-finite values.
Results may differ from a plain program's by a relative error of at most 0.0001.
Values sent between devices are 32-bit elements; how exact they have to be, the bound alone decides.
A program may use at most 64 MiB of HBM per device.

v0:
```python
import jax
import jax.numpy as jnp
from jax import lax
from jax.sharding import PartitionSpec as P

D = 8192
ROWS = 32
MB = 32


EPSILON = 1e-06


def shifted(array, axis, by):
    count = lax.axis_size(axis)
    pairs = [(i, i + by) for i in range(count) if 0 <= i + by < count]
    return lax.ppermute(array, axis, pairs)


def advance(site_piece, env_cols, scale, outcome):
    slots = env_cols.shape[1]
    term = jnp.einsum(
        "slr,lm->rsm",
        site_piece,
        env_cols,
        precision=lax.Precision.HIGHEST,
        preferred_element_type=jnp.float32,
    )
    shard = lax.psum_scatter(
        term.reshape(lax.axis_size("bond") * site_piece.shape[1], 2 * slots),
        "bond",
        scatter_dimension=0,
        tiled=True,
    )
    amps = shard.reshape(shard.shape[0], 2, slots)
    local_sq = jnp.sum(amps * amps, axis=0)
    totals = lax.psum(local_sq, "bond")
    means = totals / (D * scale)[None, :] + EPSILON
    picked = outcome == 1
    chosen = jnp.where(picked[None, :], amps[:, 1, :], amps[:, 0, :])
    weight = jnp.where(picked, means[1], means[0])
    probs = weight / (means[0] + means[1])
    env_next = chosen * lax.rsqrt(scale * weight)[None, :]
    scale_next = jnp.ones_like(scale)
    return (env_next, scale_next, probs)


def on_device(sites, boundary, bits, order):
    group = lax.axis_index("seg")
    sections = lax.axis_size("seg")
    block = MB
    count = ROWS // block
    steps = count + sections - 1
    slot_bits = jnp.take(bits, order, axis=0)
    local_width = sites.shape[2]
    start_env = jnp.broadcast_to(boundary[:, None], (local_width, block))
    unit_scale = jnp.ones((block,), jnp.float32)

    def one_step(step, carry):
        env_in, scale_in, table = carry
        batch = step - group
        valid = jnp.logical_and(batch >= 0, batch < count)
        clipped = jnp.clip(batch, 0, count - 1)
        first = group == 0
        env_cols = jnp.where(first, start_env, env_in)
        scale = jnp.where(first, unit_scale, scale_in)
        env_cols, scale, probs = advance(sites[0], env_cols, scale, slot_bits[:, 0])
        columns = [probs]
        block_probs = jnp.stack(columns, axis=1)
        updated = lax.dynamic_update_slice(table, block_probs, (clipped * block, jnp.int32(0)))
        table = jnp.where(valid, updated, table)
        env_out = shifted(env_cols, "seg", 1)
        return (env_out, scale, table)

    table_init = jnp.zeros((ROWS, sites.shape[0]), jnp.float32)
    env_init = jnp.zeros((local_width, block), jnp.float32)
    final = lax.fori_loop(0, steps, one_step, (env_init, unit_scale, table_init))
    return final[2]


def solution(mesh):
    return jax.shard_map(
        on_device,
        mesh=mesh,
        in_specs=(P("seg", None, "bond", None), P("bond"), P(None, "seg"), P()),
        out_specs=P(None, "seg"),
        check_vma=False,
    )
```

profile of v0, /device:TPU:24, one launch (start us, length us, event | category | flops | bytes accessed | tf_op | source)
XLA Modules:
  0.0 1133.9 jit_solution(4633171038704699626)
XLA Ops:
  8.6 1118.2 %while.17 = (s32[]{:T(128)}, f32[128,32]{0,1:T(8,128)S(1)}, f32[32,1]{0,1:T(1,128)S(1)}, s32[32,1]{0,1:T(1,128)S(1)}, pred[]{:T(512)}, /*index=5*/f32[1,2,128,81...) while((s32[]{:T(128)}, f32[128,32]{0,1:T(8,128)S(1)}, f32[32,1]{0,1:T(1,128)S(1)}, ...), condition=%wide.region_4.5_spmd.clone, body=%wide.region_0.4_spmd.clone.sunk | while | flops 805335488 | bytes 17043360 | solution.py:77
  8.6 7.7 fusion.23
  16.4 144.3 %reduce-scatter.2.cloned.1.call-done = f32[128,64]{0,1:T(8,128)} async-done(((f32[8192,64]{0,1:T(8,128)}), f32[128,64]{0,1:T(8,128)}) %reduce-scatter.2.cloned.1.call-update) | async-done | bytes 32784 | tf_op jit(solution)/shard_map/while/body/eval_jaxpr/reduce_scatter | solution.py:29
  160.7 0.9 multiply_reduce_fusion.2
  161.7 124.0 %psum.14 = f32[2,32]{1,0:T(2,128)S(1)} all-reduce(f32[2,32]{1,0:T(2,128)S(1)} %reduce_sum.19), channel_id=1, replica_groups=mesh['seg'=4,'bond'=64] {'bond'}, use_global_device_ids=true, to_apply=%region_3.3 | all-reduce | flops 64 | bytes 512 | tf_op jit(solution)/shard_map/while/body/eval_jaxpr/psum | solution.py:37
  286.6 1.3 collective-permute-start
  287.9 4.3 collective-permute-done
  292.2 7.7 fusion.23
  299.9 139.0 %reduce-scatter.2.cloned.1.call-done = f32[128,64]{0,1:T(8,128)} async-done(((f32[8192,64]{0,1:T(8,128)}), f32[128,64]{0,1:T(8,128)}) %reduce-scatter.2.cloned.1.call-update) | async-done | bytes 32784 | tf_op jit(solution)/shard_map/while/body/eval_jaxpr/reduce_scatter | solution.py:29
  438.9 0.9 multiply_reduce_fusion.2
  439.9 124.0 %psum.14 = f32[2,32]{1,0:T(2,128)S(1)} all-reduce(f32[2,32]{1,0:T(2,128)S(1)} %reduce_sum.19), channel_id=1, replica_groups=mesh['seg'=4,'bond'=64] {'bond'}, use_global_device_ids=true, to_apply=%region_3.3 | all-reduce | flops 64 | bytes 512 | tf_op jit(solution)/shard_map/while/body/eval_jaxpr/psum | solution.py:37
  564.8 1.3 collective-permute-start
  566.1 4.3 collective-permute-done
  570.4 7.7 fusion.23
  578.1 139.0 %reduce-scatter.2.cloned.1.call-done = f32[128,64]{0,1:T(8,128)} async-done(((f32[8192,64]{0,1:T(8,128)}), f32[128,64]{0,1:T(8,128)}) %reduce-scatter.2.cloned.1.call-update) | async-done | bytes 32784 | tf_op jit(solution)/shard_map/while/body/eval_jaxpr/reduce_scatter | solution.py:29
  717.1 0.9 multiply_reduce_fusion.2
  718.1 124.0 %psum.14 = f32[2,32]{1,0:T(2,128)S(1)} all-reduce(f32[2,32]{1,0:T(2,128)S(1)} %reduce_sum.19), channel_id=1, replica_groups=mesh['seg'=4,'bond'=64] {'bond'}, use_global_device_ids=true, to_apply=%region_3.3 | all-reduce | flops 64 | bytes 512 | tf_op jit(solution)/shard_map/while/body/eval_jaxpr/psum | solution.py:37
  842.9 1.3 collective-permute-start
  844.3 4.3 collective-permute-done
  848.6 7.7 fusion.23
  856.3 139.1 %reduce-scatter.2.cloned.1.call-done = f32[128,64]{0,1:T(8,128)} async-done(((f32[8192,64]{0,1:T(8,128)}), f32[128,64]{0,1:T(8,128)}) %reduce-scatter.2.cloned.1.call-update) | async-done | bytes 32784 | tf_op jit(solution)/shard_map/while/body/eval_jaxpr/reduce_scatter | solution.py:29
  996.3 124.0 %psum.14 = f32[2,32]{1,0:T(2,128)S(1)} all-reduce(f32[2,32]{1,0:T(2,128)S(1)} %reduce_sum.19), channel_id=1, replica_groups=mesh['seg'=4,'bond'=64] {'bond'}, use_global_device_ids=true, to_apply=%region_3.3 | all-reduce | flops 64 | bytes 512 | tf_op jit(solution)/shard_map/while/body/eval_jaxpr/psum | solution.py:37
  1121.2 1.3 collective-permute-start
  1122.5 4.3 collective-permute-done
  (43 shorter events, 7.3 us)
Async XLA Ops:
  6.5 0.7 copy-start
  8.6 152.1 %reduce-scatter.2.cloned.1.call-start = ((), (), s32[]{:S(2)}) async-start(), calls=%async_computation.1 | async-start | bytes 2129920 | tf_op jit(solution)/shard_map/while/body/eval_jaxpr/reduce_scatter | solution.py:29
  286.6 5.6 collective-permute-start
  292.2 146.7 %reduce-scatter.2.cloned.1.call-start = ((), (), s32[]{:S(2)}) async-start(), calls=%async_computation.1 | async-start | bytes 2129920 | tf_op jit(solution)/shard_map/while/body/eval_jaxpr/reduce_scatter | solution.py:29
  564.8 5.6 collective-permute-start
  570.4 146.7 %reduce-scatter.2.cloned.1.call-start = ((), (), s32[]{:S(2)}) async-start(), calls=%async_computation.1 | async-start | bytes 2129920 | tf_op jit(solution)/shard_map/while/body/eval_jaxpr/reduce_scatter | solution.py:29
  842.9 5.6 collective-permute-start
  848.6 146.8 %reduce-scatter.2.cloned.1.call-start = ((), (), s32[]{:S(2)}) async-start(), calls=%async_computation.1 | async-start | bytes 2129920 | tf_op jit(solution)/shard_map/while/body/eval_jaxpr/reduce_scatter | solution.py:29
  1121.2 5.6 collective-permute-start
  1126.8 0.5 copy-start.1
Sparse Core Ops, SparseCore 0:
  16.5 144.2 reduce-scatter.1
  300.0 138.8 reduce-scatter.1
  578.2 138.8 reduce-scatter.1
  856.4 138.9 reduce-scatter.1
where the time goes:
time: 1140 us; the launch traced here: 1130 us
  waiting for transfers between devices  579 us (51%)
  blocking collectives  496 us (44%)
  matrix products  30.8 us (3%)
  between operations  13.1 us (1%)
    reduce_scatter x4, waiting for transfers between devices, advance(): lax.psum_scatter(term.reshape(lax.axis_size('bond') * site_piece.shape[1]...  561 us
    psum x4, blocking collectives, advance(): totals = lax.psum(local_sq, 'bond')  496 us
    dot_general x4, matrix products, advance(): jnp.einsum('slr,lm->rsm', site_piece, env_cols, precision=lax.Precision.H...  30.8 us
  transfers between devices with their start and end apart: 8, of which 8 were waited for; matrix products, arithmetic and copies ran while one was open for 0% of the time, Pallas kernels for 0%

commit v1 on v0

v1 whole, which is shorter than its diff:
```python
import functools

import jax
import jax.numpy as jnp
from jax import lax
from jax.experimental import pallas as pl
from jax.experimental.pallas import tpu as pltpu
from jax.sharding import PartitionSpec as P

EPSILON = 1e-06
LANES = 128
SEGS = 4
MXU_FROM = 2


def grouping(bonds):
    ng = 8 if bonds == 64 else 2
    return bonds // ng, ng


def group_orders(ng):
    nx = ng // 2
    far = sorted(range(nx), key=lambda d: -min(d, nx - d))
    pairs = [(dx, dc) for dx in far if dx for dc in (0, 1)]
    return pairs + [(0, 1), (0, 0)]


def ring_order(n):
    return sorted(range(n), key=lambda d: -min(d, n - d))


def lookup(t, table):
    value = jnp.int32(table[0])
    for i, entry in enumerate(table):
        if i:
            value = jnp.where(t == i, jnp.int32(entry), value)
    return value


def lane_iota(rows):
    return lax.broadcasted_iota(jnp.int32, (rows, LANES), 1)


def row_iota(rows):
    return lax.broadcasted_iota(jnp.int32, (rows, LANES), 0)


def column_of(row, rows):
    hit = lane_iota(rows) == row_iota(rows)
    zero = jnp.zeros((), row.dtype)
    return jnp.sum(jnp.where(hit, jnp.broadcast_to(row, (rows, LANES)), zero), axis=1, keepdims=True)


def row_of(column, offset):
    rows = column.shape[0]
    hit = lane_iota(rows) == row_iota(rows) + offset
    return jnp.sum(jnp.where(hit, jnp.broadcast_to(column, (rows, LANES)), 0.0), axis=0, keepdims=True)


def level_offset(k):
    return 2 ** (k + 1) - 2


def kernel(
    nz, ng, slots, dim,
    sites, boundary, bits, order, out,
    tile, split, envs,
    pa0, pa1, pa2, pa3, ra0, ra1, ra2, ra3,
    pb0, pb1, pb2, pb3, rb0, rb1, rb2, rb3,
    pe2, pe3, re2, re3,
    fs, fr, s1, r1, s2, r2,
    load_sem, sa_sem, ra_sem, sb_sem, rb_sem, se_sem, re_sem, rb3_sem, re3_sem, f_sem, fr_sem, s1_sem, r1_sem, s2_sem, r2_sem,
):
    pa, ra = (pa0, pa1, pa2, pa3), (ra0, ra1, ra2, ra3)
    pb, rb = (pb0, pb1, pb2, pb3), (rb0, rb1, rb2, rb3)
    pe, re = (None, None, pe2, pe3), (None, None, re2, re3)
    last = SEGS - 1
    seg, bond = lax.axis_index("seg"), lax.axis_index("bond")
    z_me, g_me = lax.div(bond, ng), lax.rem(bond, ng)
    x_me, c_me = lax.div(g_me, 2), lax.rem(g_me, 2)
    pairs = group_orders(ng)
    bonds = nz * ng
    width = tile.shape[2]

    def member(dx, dc):
        return lax.rem(x_me + dx, ng // 2) * 2 + lax.rem(c_me + dc, 2)

    def remote(src, dst, send, recv, to_seg, to_bond):
        return pltpu.make_async_remote_copy(
            src_ref=src, dst_ref=dst, send_sem=send, recv_sem=recv,
            device_id={"seg": to_seg, "bond": to_bond}, device_id_type=pl.DeviceIdType.MESH,
        )

    def wait_bytes(ref, sem):
        pltpu.make_async_copy(ref, ref, sem).wait()

    def load(t):
        g = member(lookup(t, [p[0] for p in pairs]), lookup(t, [p[1] for p in pairs]))
        for z in range(nz):
            start = pl.multiple_of((z * ng + g) * width, width)
            pltpu.make_async_copy(
                sites.at[0, :, :, pl.ds(start, width)],
                tile.at[g, :, :, pl.ds(z * width, width)],
                load_sem.at[t],
            ).start()

    pl.loop(0, ng)(load)

    barrier = pltpu.get_barrier_semaphore()

    def hello(to_seg, to_bond):
        pl.semaphore_signal(
            barrier, inc=1, device_id={"seg": to_seg, "bond": to_bond}, device_id_type=pl.DeviceIdType.MESH
        )

    for dx, dc in pairs[:-1]:
        hello(seg, z_me * ng + member(dx, dc))

    @pl.when(seg > 0)
    def _():
        for d in ring_order(nz):
            hello(seg - 1, lax.rem(z_me + d, nz) * ng + g_me)

    @pl.when(seg == last)
    def _():
        for d in ring_order(nz)[:-1]:
            hello(seg, lax.rem(z_me + d, nz) * ng + g_me)

    @pl.when(seg < last)
    def _():
        hello(last, bond)

    bits_row = row_of(bits[...].astype(jnp.float32), 0)
    order_column = column_of(order[...], slots)

    def group_of(t):
        dx, dc = lookup(t, [p[0] for p in pairs]), lookup(t, [p[1] for p in pairs])
        return member(dx, dc), dx * 2 + dc - 1

    def wait_tile(t, g):
        wait_bytes(tile.at[g], load_sem.at[t])

    @pl.when(seg >= MXU_FROM)
    def _():
        @pl.loop(0, ng)
        def _(t):
            g, _slot = group_of(t)
            wait_tile(t, g)
            for s in range(2):
                a = tile[g, s]
                high = a.astype(jnp.bfloat16)
                low = (a - high.astype(jnp.float32)).astype(jnp.bfloat16)
                span = pl.ds(s * nz * width, nz * width)
                split[g, 0:width, span] = high
                split[g, width : 2 * width, span] = low

    @pl.when(seg < last)
    def _():
        pl.semaphore_wait(barrier, ng - 1 + nz)

    @pl.when(seg == last)
    def _():
        pl.semaphore_wait(barrier, ng - 1 + nz - 1 + last)

    def probabilities(totals, row_bits):
        lanes = lane_iota(slots)
        table = jnp.broadcast_to(totals, (slots, LANES))
        node = jnp.zeros((slots, 1), jnp.int32)
        scale = jnp.full((slots, 1), float(dim), jnp.float32)
        answer = jnp.zeros((slots, 1), jnp.float32)

        def pick(where_lane, source):
            return jnp.sum(jnp.where(lanes == where_lane, source, 0.0), axis=1, keepdims=True)

        for k in range(SEGS):
            if k < last:
                bit = pick(order_column + (32 + slots * k), table)
            else:
                bit = pick(order_column, jnp.broadcast_to(row_bits, (slots, LANES)))
            chosen = (bit > 0.5).astype(jnp.int32)
            base = level_offset(k) + node
            m_chosen = pick(base + chosen * 2**k, table) / scale + EPSILON
            m_other = pick(base + (1 - chosen) * 2**k, table) / scale + EPSILON
            answer = jnp.where(seg == k, m_chosen / (m_chosen + m_other), answer)
            scale = scale * m_chosen
            node = node + chosen * 2**k
        return answer

    for k in range(SEGS):
        rows_in = 2**k
        rows_out = 2 * rows_in
        embed = pe[k] is None

        @pl.when(seg == k)
        def _(k=k, rows_in=rows_in, rows_out=rows_out, embed=embed):
            if k == 0:
                env = boundary[...]
                extra = row_of(bits[...].astype(jnp.float32), 32) / bonds
            else:
                source = rb[k - 1]
                wait_bytes(source, rb_sem)
                env = source[0, 0:rows_in, :]
                for d in range(1, nz):
                    env = env + source[d, 0:rows_in, :]
                if pe[k - 1] is None:
                    extra = source[0, rows_in : rows_in + 1, :]
                    for d in range(1, nz):
                        extra = extra + source[d, rows_in : rows_in + 1, :]
                else:
                    wait_bytes(re[k - 1], re_sem)
                    extra = re[k - 1][0]
                    for d in range(1, nz):
                        extra = extra + re[k - 1][d]
                extra = extra / bonds + row_of(jnp.sum(env * env, axis=1, keepdims=True), level_offset(k - 1))
                if k < last:
                    extra = extra + row_of(bits[...].astype(jnp.float32), 32 + slots * k) / bonds

            if k < MXU_FROM:
                for j in range(rows_in):
                    envs[j] = jnp.broadcast_to(column_of(env[j : j + 1, :], width), (width, width))
            else:
                if rows_in < 8:
                    env = jnp.concatenate([env, jnp.zeros((8 - rows_in, width), jnp.float32)], axis=0)
                high = env.astype(jnp.bfloat16).astype(jnp.float32)
                both = jnp.concatenate([high, env - high], axis=0).astype(jnp.bfloat16)
                left = jnp.concatenate([both, both], axis=1)
            extra8 = jnp.broadcast_to(extra, (8, LANES))

            @pl.loop(0, ng)
            def _(t):
                g, slot = group_of(t)
                if k < MXU_FROM:
                    wait_tile(t, g)
                    for z in range(nz):
                        for s in range(2):
                            a = tile[g, s, :, z * width : (z + 1) * width]
                            for j in range(rows_in):
                                row = z * rows_out + s * rows_in + j
                                pa[k][g, row : row + 1, :] = jnp.sum(a * envs[j], axis=0, keepdims=True)
                else:
                    product = jnp.dot(left, split[g], preferred_element_type=jnp.float32)
                    product = product[0:8] + product[8:16]
                    for z in range(nz):
                        for s in range(2):
                            row = z * rows_out + s * rows_in
                            column = (s * nz + z) * width
                            pa[k][g, row : row + rows_in, :] = product[0:rows_in, column : column + width]
                pa[k][g, nz * rows_out : nz * rows_out + 8, :] = extra8

                @pl.when(t < ng - 1)
                def _():
                    remote(pa[k].at[g], ra[k].at[slot], sa_sem, ra_sem, seg, z_me * ng + g).start()

            wait_bytes(ra[k], ra_sem)
            for z in range(nz):
                rows = slice(z * rows_out, (z + 1) * rows_out)
                total = pa[k][g_me, rows, :]
                for i in range(ng - 1):
                    total = total + ra[k][i, rows, :]
                pb[k][z, 0:rows_out, :] = total
            rows = slice(nz * rows_out, nz * rows_out + 8)
            total = pa[k][g_me, rows, :]
            for i in range(ng - 1):
                total = total + ra[k][i, rows, :]
            if embed:
                for z in range(nz):
                    pb[k][z, rows_out : 2 * rows_out, :] = total[0:rows_out]
            else:
                pe[k][...] = total[0:1]

            to_seg = seg + 1 if k < last else seg
            data_sem, extra_sem = (rb_sem, re_sem) if k < last else (rb3_sem, re3_sem)
            for d in ring_order(nz):
                if k == last and d == 0:
                    continue
                z = lax.rem(z_me + d, nz)
                slot = d if k < last else d - 1
                to_bond = z * ng + g_me
                remote(pb[k].at[z], rb[k].at[slot], sb_sem, data_sem, to_seg, to_bond).start()
                if not embed:
                    remote(pe[k], re[k].at[slot], se_sem, extra_sem, to_seg, to_bond).start()

            if k < last:
                wait_bytes(fr, fr_sem)
                out[...] = probabilities(fr[...], bits_row)
            else:
                wait_bytes(rb[k], rb3_sem)
                final = pb[k][z_me]
                for d in range(nz - 1):
                    final = final + rb[k][d]
                s1[...] = row_of(jnp.sum(final * final, axis=1, keepdims=True), level_offset(k))
                for dx, dc in pairs[:-1]:
                    remote(
                        s1, r1.at[dx * 2 + dc - 1], s1_sem, r1_sem, seg, z_me * ng + member(dx, dc)
                    ).start()
                wait_bytes(re[k], re3_sem)
                known = pe[k][...]
                for d in range(nz - 1):
                    known = known + re[k][d]
                fs[...] = known
                for to in range(last):
                    remote(fs, fr, f_sem, fr_sem, to, bond).start()
                wait_bytes(r1, r1_sem)
                norms = s1[...]
                for i in range(ng - 1):
                    norms = norms + r1[i]
                s2[...] = norms
                for d in ring_order(nz)[:-1]:
                    z = lax.rem(z_me + d, nz)
                    remote(s2, r2.at[d - 1], s2_sem, r2_sem, seg, z * ng + g_me).start()
                wait_bytes(r2, r2_sem)
                for d in range(nz - 1):
                    norms = norms + r2[d]
                out[...] = probabilities(known + norms, bits_row)
                wait_bytes(r1, s1_sem)
                wait_bytes(r2, s2_sem)
                for _i in range(last):
                    wait_bytes(fs, f_sem)

            wait_bytes(ra[k], sa_sem)
            wait_bytes(rb[k], sb_sem)
            if not embed:
                wait_bytes(re[k], se_sem)


def on_device(nz, ng, sites, boundary, bits, order):
    slots = bits.shape[0]
    width = sites.shape[2]
    dim = sites.shape[3]
    f32 = jnp.float32

    def rows(k):
        return 2 ** (k + 1)

    pa = [pltpu.VMEM((ng, nz * rows(k) + 8, LANES), f32) for k in range(SEGS)]
    ra = [pltpu.VMEM((ng - 1, nz * rows(k) + 8, LANES), f32) for k in range(SEGS)]
    held = [rows(k) * (2 if k < 2 else 1) for k in range(SEGS)]
    pb = [pltpu.VMEM((nz, held[k], LANES), f32) for k in range(SEGS)]
    rb = [pltpu.VMEM((nz if k < SEGS - 1 else nz - 1, held[k], LANES), f32) for k in range(SEGS)]
    one = pltpu.VMEM((1, LANES), f32)
    dma = pltpu.SemaphoreType.DMA
    scratch = [
        pltpu.VMEM((ng, 2, width, nz * width), f32),
        pltpu.VMEM((ng, 2 * width, 2 * nz * width), jnp.bfloat16),
        pltpu.VMEM((2, width, LANES), f32),
        *pa, *ra, *pb, *rb,
        one, one,
        pltpu.VMEM((nz, 1, LANES), f32), pltpu.VMEM((nz - 1, 1, LANES), f32),
        one, one,
        one, pltpu.VMEM((ng - 1, 1, LANES), f32),
        one, pltpu.VMEM((nz - 1, 1, LANES), f32),
        dma((ng,)),
        *([dma(())] * 14),
    ]
    padded = jnp.pad(order, (0, LANES - slots)).reshape(1, LANES)
    vmem = pl.BlockSpec(memory_space=pltpu.VMEM)
    return pl.pallas_call(
        functools.partial(kernel, nz, ng, slots, dim),
        out_shape=jax.ShapeDtypeStruct((slots, 1), f32),
        in_specs=[pl.BlockSpec(memory_space=pl.ANY), vmem, vmem, vmem],
        out_specs=vmem,
        scratch_shapes=scratch,
        compiler_params=pltpu.CompilerParams(
            collective_id=0, has_side_effects=True, vmem_limit_bytes=48 * 1024 * 1024
        ),
        name="chain",
    )(sites, boundary.reshape(1, width), bits, padded)


def solution(mesh):
    nz, ng = grouping(mesh.shape["bond"])
    return jax.shard_map(
        functools.partial(on_device, nz, ng),
        mesh=mesh,
        in_specs=(P("seg", None, "bond", None), P("bond"), P(None, "seg"), P()),
        out_specs=P(None, "seg"),
        check_vma=False,
    )
```

time: 1140 us -> 59.6 us (0.05)
  waiting for transfers between devices: 579 us -> 0 us
  blocking collectives: 496 us -> 0 us
  Pallas kernels: 0 us -> 56.9 us
  matrix products: 30.8 us -> 0 us
  between operations: 13.1 us -> 0.01 us
    reduce_scatter x4 -> x0, waiting for transfers between devices: 561 us -> none  [advance(): lax.psum_scatter(term.reshape(lax.axis_size('bond') * site_piece.shape[1]...]
    psum x4 -> x0, blocking collectives: 496 us -> none  [advance(): totals = lax.psum(local_sq, 'bond')]
    pallas_call x0 -> x1, Pallas kernels: none -> 56.9 us  [on_device(): pl.pallas_call(functools.partial(kernel, nz, ng, slots, dim), out_shape=j...]
    dot_general x4 -> x0, matrix products: 30.8 us -> none  [advance(): jnp.einsum('slr,lm->rsm', site_piece, env_cols, precision=lax.Precision.H...]
    ppermute x4 -> x0, waiting for transfers between devices: 17.2 us -> none  [shifted(): return lax.ppermute(array, axis, pairs)]
  transfers between devices with their start and end apart: 8 -> 0, of which waited for: 8 -> 0; matrix products, arithmetic and copies ran while one was open for 0% -> 0% of each run, Pallas kernels for 0% -> 0%
where the time goes in v1:
time: 59.6 us; the launch traced here: 59.5 us
  Pallas kernels  56.9 us (95%)
  local copies, waits for them, and re-layouts  2.63 us (4%)
    pallas_call x1, Pallas kernels, on_device(): pl.pallas_call(functools.partial(kernel, nz, ng, slots, dim), out_shape=j...  56.9 us
    unnamed x3, local copies, waits for them, and re-layouts  1.39 us

profile of v1, /device:TPU:24, one launch (start us, length us, event | category | flops | bytes accessed | tf_op | source)
XLA Modules:
  0.0 59.5 jit_solution(13710133271801672321)
XLA Ops:
  0.0 0.7 %pad_bitcast_fusion.order = s32[1,128]{1,0:T(1,128)S(1)} fusion(s32[32]{0:T(128)} %param.7), kind=kLoop, calls=%fused_computation | loop fusion | bytes 640 | tf_op jit(solution)/shard_map/reshape | solution.py:355
  0.7 0.7 %copy.5.bits = s32[32,1]{1,0:T(8,128)S(1)} copy(s32[32,1]{0,1:T(1,128)} %param.6) | data formatting | bytes 256 | tf_op args[2]
  1.4 0.0 copy-start
  1.4 0.7 %copy-done = f32[128]{0:T(128)S(1)} copy-done((f32[128]{0:T(128)S(1)}, f32[128]{0:T(128)}, u32[]{:S(2)}) %copy-start) | copy-done | bytes 536
  2.0 56.9 %chain.1 = f32[32,1]{1,0:T(8,128)S(1)} custom-call(f32[1,2,128,8192]{3,2,1,0:T(8,128)} %sites.1, f32[1,128]{1,0:T(1,128)S(1)} %bitcast.3, s32[32,1]{1,0:T(8,128)S(1)} %copy.5.bits, s32[1,128]{1,0:T(1,128)S(1)} %pad_bitcast_fusion.order), custom_call_target="tpu_custom_call" | custom-call | tf_op jit(solution)/shard_map/chain/pallas_call | solution.py:357
  59.0 0.6 copy.6
Async XLA Ops:
  1.4 0.7 %copy-start = (f32[128]{0:T(128)S(1)}, f32[128]{0:T(128)}, u32[]{:S(2)}) copy-start(f32[128]{0:T(128)} %param.5) | copy-start | bytes 1540

commit v2 on v0

v2 whole, which is shorter than its diff:
```python
import functools

import jax
import jax.numpy as jnp
from jax import lax
from jax.experimental import pallas as pl
from jax.experimental.pallas import tpu as pltpu
from jax.sharding import PartitionSpec as P

EPSILON = 1e-06
LANES = 128
SEGS = 4
MESH = pl.DeviceIdType.MESH


def grouping(bonds):
    return (8, 4) if bonds == 64 else (bonds // 2, 1)


def far_first(n):
    return sorted(range(n), key=lambda d: -min(d, n - d))


def lookup(t, table):
    value = jnp.int32(table[0])
    for i, entry in enumerate(table):
        if i:
            value = jnp.where(t == i, jnp.int32(entry), value)
    return value


def iota(shape, axis):
    return lax.broadcasted_iota(jnp.int32, shape, axis)


def column_of(row, rows):
    shape = (rows, row.shape[1])
    hit = iota(shape, 1) == iota(shape, 0)
    zero = jnp.zeros((), row.dtype)
    return jnp.sum(jnp.where(hit, jnp.broadcast_to(row, shape), zero), axis=1, keepdims=True)


def row_of(column, offset, lanes=LANES):
    shape = (column.shape[0], lanes)
    hit = iota(shape, 1) == iota(shape, 0) + offset
    return jnp.sum(jnp.where(hit, jnp.broadcast_to(column, shape), 0.0), axis=0, keepdims=True)


def total_of(ref, count, rows):
    chains = [ref[i, rows, :] for i in range(min(4, count))]
    for i in range(4, count):
        chains[i % 4] = chains[i % 4] + ref[i, rows, :]
    while len(chains) > 1:
        chains = [sum(chains[i + 1 : i + 2], chains[i]) for i in range(0, len(chains), 2)]
    return chains[0]


def level_offset(k):
    return 2 ** (k + 1) - 2


def kernel(
    nz, nx, slots, dim,
    sites, boundary_hbm, bits_hbm, order_hbm, out,
    tile, split, env0, boundary, bits, order,
    pp1, pp2, pp3, rp1, rp2, rp3,
    pb0, pb1, pb2, pb3, rb0, rb1, rb2, rb3,
    fs, fr, s1, r1,
    load_sem, small_sem, sp_sem, rp_sem, sb_sem, rb_sem, rb3_sem, f_sem, fr_sem, s1_sem, r1_sem,
):
    pp, rp = (None, pp1, pp2, pp3), (None, rp1, rp2, rp3)
    pb, rb = (pb0, pb1, pb2, pb3), (rb0, rb1, rb2, rb3)
    last = SEGS - 1
    bonds, ng = nz * nx * 2, nx * 2
    width = tile.shape[2]
    seg, bond = lax.axis_index("seg"), lax.axis_index("bond")
    z_me, g_me = lax.div(bond, ng), lax.rem(bond, ng)
    x_me, c_me = lax.div(g_me, 2), lax.rem(g_me, 2)
    partner = lax.rem(c_me + 1, 2)
    xs = far_first(nx)
    chips = [(dz, dx) for dz in far_first(nz) for dx in xs]

    def at(dz, dx, core):
        return (lax.rem(z_me + dz, nz) * nx + lax.rem(x_me + dx, nx)) * 2 + core

    def remote(src, dst, send, recv, to_seg, to_bond):
        return pltpu.make_async_remote_copy(
            src_ref=src, dst_ref=dst, send_sem=send, recv_sem=recv,
            device_id={"seg": to_seg, "bond": to_bond}, device_id_type=MESH,
        )

    def wait_bytes(ref, sem):
        pltpu.make_async_copy(ref, ref, sem).wait()

    barrier = pltpu.get_barrier_semaphore()

    def hello(to_seg, to_bond):
        pl.semaphore_signal(barrier, inc=1, device_id={"seg": to_seg, "bond": to_bond}, device_id_type=MESH)

    @pl.when(seg == 1)
    def _():
        for dz, dx in chips:
            for core in (0, 1):
                hello(0, at(dz, dx, core))

    @pl.when(seg >= 2)
    def _():
        for dz, dx in chips:
            hello(seg - 1, at(dz, dx, c_me))

    @pl.when(seg == last)
    def _():
        for dz, dx in chips:
            hello(seg, at(dz, dx, partner))
            if dz or dx:
                hello(seg, at(dz, dx, c_me))

    @pl.when(seg < last)
    def _():
        hello(last, bond)

    @pl.when(jnp.logical_and(seg > 0, seg < last))
    def _():
        hello(seg, at(0, 0, partner))

    small = [
        pltpu.make_async_copy(src, dst, small_sem.at[i])
        for i, (src, dst) in enumerate(((boundary_hbm, boundary), (bits_hbm, bits), (order_hbm, order)))
    ]
    for copy in small:
        copy.start()

    def piece(t):
        dx = lookup(t, xs + xs)
        return lax.rem(x_me + dx, nx) * 2 + jnp.where(t < nx, partner, c_me)

    @pl.loop(0, ng)
    def _(t):
        g = piece(t)
        for z in range(nz):
            start = pl.multiple_of((z * ng + g) * width, width)
            pltpu.make_async_copy(
                sites.at[0, :, :, pl.ds(start, width)],
                tile.at[g, :, :, pl.ds(z * width, width)],
                load_sem.at[t],
            ).start()

    for copy in small:
        copy.wait()
    bits_row = bits[...].astype(jnp.float32)
    order_column = column_of(order[...], slots)

    def bits_at(k):
        parts = [jnp.zeros((1, slots), jnp.float32)] * (LANES // slots)
        parts[k + 1] = bits_row
        return jnp.concatenate(parts, axis=1)

    @pl.when(seg == 0)
    def _():
        extra = bits_at(0) / bonds
        env0[...] = jnp.broadcast_to(column_of(boundary[...], width), (width, LANES))

        @pl.loop(0, ng)
        def _(t):
            g = piece(t)
            wait_bytes(tile.at[g], load_sem.at[t])
            for z in range(nz):
                for s in range(2):
                    a = tile[g, s, :, z * width : (z + 1) * width]
                    pb0[g * nz + z, s : s + 1, :] = jnp.sum(a * env0[...], axis=0, keepdims=True)
                pb0[g * nz + z, 2:3, :] = extra

    @pl.when(seg > 0)
    def _():
        @pl.loop(0, ng)
        def _(t):
            g = piece(t)
            wait_bytes(tile.at[g], load_sem.at[t])
            for s in range(2):
                a = tile[g, s]
                high = a.astype(jnp.bfloat16)
                low = (a - high.astype(jnp.float32)).astype(jnp.bfloat16)
                span = pl.ds(s * nz * width, nz * width)
                split[g, 0:width, span] = high
                split[g, width : 2 * width, span] = low

    @pl.when(seg == 0)
    def _():
        pl.semaphore_wait(barrier, bonds)

    @pl.when(jnp.logical_and(seg > 0, seg < last))
    def _():
        pl.semaphore_wait(barrier, 1 + nz * nx)

    @pl.when(seg == last)
    def _():
        pl.semaphore_wait(barrier, bonds - 1 + last)

    lanes = iota((slots, LANES), 1)

    def pick(where_lane, source):
        return jnp.sum(jnp.where(lanes == where_lane, source, 0.0), axis=1, keepdims=True)

    def site_probability(k, table, bit, node, scale):
        chosen = (bit > 0.5).astype(jnp.int32)
        base = level_offset(k) + node
        m_chosen = pick(base + chosen * 2**k, table) / scale + EPSILON
        m_other = pick(base + (1 - chosen) * 2**k, table) / scale + EPSILON
        return m_chosen / (m_chosen + m_other), node + chosen * 2**k, scale * m_chosen

    def early_sites(known):
        table = jnp.broadcast_to(known, (slots, LANES))
        state = (jnp.zeros((slots, 1), jnp.int32), jnp.full((slots, 1), float(dim), jnp.float32))
        answer = jnp.zeros((slots, 1), jnp.float32)
        for k in range(last):
            bit = pick(order_column + slots * (k + 1), table)
            probability, *state = site_probability(k, table, bit, *state)
            answer = jnp.where(seg == k, probability, answer)
        return answer, state

    def receive(k):
        count = bonds if k == 1 else nz * nx
        rows = 2**k
        wait_bytes(rb[k - 1], rb_sem)
        env = total_of(rb[k - 1], count, slice(0, rows))
        extra = total_of(rb[k - 1], count, slice(rows, rows + 1)) / bonds
        return env, extra

    def advance(k):
        rows_in, rows_out = 2**k, 2 ** (k + 1)
        block = nz * rows_out
        env, extra = receive(k)
        env8 = env
        if rows_in < 8:
            env8 = jnp.concatenate([env, jnp.zeros((8 - rows_in, width), jnp.float32)], axis=0)
        high = env8.astype(jnp.bfloat16).astype(jnp.float32)
        both = jnp.concatenate([high, env8 - high], axis=0).astype(jnp.bfloat16)
        left = jnp.concatenate([both, both], axis=1)
        extra = extra + row_of(jnp.sum(env * env, axis=1, keepdims=True), level_offset(k - 1))
        if k < last:
            extra = extra + bits_at(k) / bonds

        def product(x, core):
            value = jnp.dot(left, split[x * 2 + core], preferred_element_type=jnp.float32)
            return value[0:8] + value[8:16]

        for t, dx in enumerate(xs):
            x = lax.rem(x_me + dx, nx)
            value = product(x, partner)
            for z in range(nz):
                for s in range(2):
                    row, column = z * rows_out + s * rows_in, (s * nz + z) * width
                    pp[k][t, row : row + rows_in, :] = value[0:rows_in, column : column + width]
            pp[k][t, block : block + 8, :] = jnp.broadcast_to(extra, (8, LANES))
            remote(pp[k].at[t], rp[k].at[t], sp_sem, rp_sem.at[t], seg, at(0, 0, partner)).start()

        to_seg = seg + 1 if k < last else seg
        recv = rb_sem if k < last else rb3_sem
        for t, dx in enumerate(xs):
            x = lax.rem(x_me + dx, nx)
            value = product(x, c_me)
            wait_bytes(rp[k].at[t], rp_sem.at[t])
            if t == 0:
                extra = extra + rp[k][t, block : block + 1, :]
            for z in range(nz):
                for s in range(2):
                    row, column = z * rows_out + s * rows_in, (s * nz + z) * width
                    pb[k][t * nz + z, s * rows_in : (s + 1) * rows_in, :] = (
                        value[0:rows_in, column : column + width] + rp[k][t, row : row + rows_in, :]
                    )
                pb[k][t * nz + z, rows_out : rows_out + 1, :] = extra
            for dz in far_first(nz):
                if k == last and dz == 0 and dx == 0:
                    continue
                slot = dz * nx + dx - (1 if k == last else 0)
                z = lax.rem(z_me + dz, nz)
                remote(pb[k].at[t * nz + z], rb[k].at[slot], sb_sem, recv, to_seg, at(dz, dx, c_me)).start()

    def drain(k):
        if k:
            wait_bytes(rp[k], sp_sem)
        wait_bytes(rb[k], sb_sem)

    @pl.when(seg == 0)
    def _():
        for dz, dx in chips:
            for core in (0, 1):
                to = at(dz, dx, core)
                mine = lax.rem(to, ng) * nz + lax.div(to, ng)
                remote(pb0.at[mine], rb0.at[(dz * nx + dx) * 2 + lax.rem(c_me + core, 2)], sb_sem, rb_sem, 1, to).start()

    for k in range(1, SEGS):
        pl.when(seg == k)(functools.partial(advance, k))

    @pl.when(seg < last)
    def _():
        wait_bytes(fr, fr_sem)
        answer, _state = early_sites(fr[...])
        out[...] = row_of(answer, 0, slots)

    for k in range(last):
        pl.when(seg == k)(functools.partial(drain, k))

    @pl.when(seg == last)
    def _():
        k, rows = last, 2 ** (last + 1)
        own = xs.index(0) * nz + z_me
        wait_bytes(rb[k], rb3_sem)
        env = pb[k][own, 0:rows, :] + total_of(rb[k], nz * nx - 1, slice(0, rows))
        s1[...] = row_of(jnp.sum(env * env, axis=1, keepdims=True), level_offset(k))
        for dz, dx in chips:
            for dc in (1, 0):
                if dz or dx or dc:
                    core = lax.rem(c_me + dc, 2)
                    remote(s1, r1.at[(dz * nx + dx) * 2 + dc - 1], s1_sem, r1_sem, seg, at(dz, dx, core)).start()
        known = pb[k][own, rows : rows + 1, :] + total_of(rb[k], nz * nx - 1, slice(rows, rows + 1))
        fs[...] = known
        for to in range(last):
            remote(fs, fr, f_sem, fr_sem, to, bond).start()
        _answer, state = early_sites(known)
        bit = pick(order_column, jnp.concatenate([bits_row] * (LANES // slots), axis=1))
        wait_bytes(r1, r1_sem)
        norms = s1[...] + total_of(r1, bonds - 1, slice(0, 1))
        probability, *_state = site_probability(k, jnp.broadcast_to(norms, (slots, LANES)), bit, *state)
        out[...] = row_of(probability, 0, slots)
        wait_bytes(r1, s1_sem)
        for _i in range(last):
            wait_bytes(fs, f_sem)
        drain(k)


def on_device(nz, nx, sites, boundary, bits, order):
    slots = bits.shape[0]
    width, dim = sites.shape[2], sites.shape[3]
    f32, i32 = jnp.float32, jnp.int32
    bonds, ng = nz * nx * 2, nx * 2
    rows = [2 ** (k + 1) for k in range(SEGS)]
    pieces = [pltpu.VMEM((nx, nz * rows[k] + 8, LANES), f32) for k in range(1, SEGS)]
    sends = [pltpu.VMEM((nz * nx * (1 if k else 2), rows[k] + 1, LANES), f32) for k in range(SEGS)]
    counts = [bonds, nz * nx, nz * nx, nz * nx - 1]
    receives = [pltpu.VMEM((counts[k], rows[k] + 1, LANES), f32) for k in range(SEGS)]
    one = pltpu.VMEM((1, LANES), f32)
    dma = pltpu.SemaphoreType.DMA
    scratch = [
        pltpu.VMEM((ng, 2, width, nz * width), f32),
        pltpu.VMEM((ng, 2 * width, 2 * nz * width), jnp.bfloat16),
        pltpu.VMEM((width, LANES), f32),
        pltpu.VMEM((1, width), f32), pltpu.VMEM((1, slots), i32), pltpu.VMEM((1, slots), i32),
        *pieces, *pieces, *sends, *receives,
        one, one, one, pltpu.VMEM((bonds - 1, 1, LANES), f32),
        dma((ng,)), dma((3,)), dma(()), dma((nx,)), *([dma(())] * 7),
    ]
    hbm = pl.BlockSpec(memory_space=pltpu.HBM)
    answer = pl.pallas_call(
        functools.partial(kernel, nz, nx, slots, dim),
        out_shape=jax.ShapeDtypeStruct((1, slots), f32),
        in_specs=[hbm] * 4,
        out_specs=pl.BlockSpec(memory_space=pltpu.VMEM),
        scratch_shapes=scratch,
        compiler_params=pltpu.CompilerParams(
            collective_id=0, has_side_effects=True, vmem_limit_bytes=67043328
        ),
        name="chain",
    )(sites, boundary.reshape(1, width), bits.T, order.reshape(1, slots))
    return answer.T


def solution(mesh):
    nz, nx = grouping(mesh.shape["bond"])
    return jax.shard_map(
        functools.partial(on_device, nz, nx),
        mesh=mesh,
        in_specs=(P("seg", None, "bond", None), P("bond"), P(None, "seg"), P()),
        out_specs=P(None, "seg"),
        check_vma=False,
    )
```

time: 1140 us -> 50.7 us (0.04)
  waiting for transfers between devices: 579 us -> 0 us
  blocking collectives: 496 us -> 0 us
  Pallas kernels: 0 us -> 49.5 us
  matrix products: 30.8 us -> 0 us
  between operations: 13.1 us -> 0.01 us
    reduce_scatter x4 -> x0, waiting for transfers between devices: 561 us -> none  [advance(): lax.psum_scatter(term.reshape(lax.axis_size('bond') * site_piece.shape[1]...]
    psum x4 -> x0, blocking collectives: 496 us -> none  [advance(): totals = lax.psum(local_sq, 'bond')]
    pallas_call x0 -> x1, Pallas kernels: none -> 49.5 us  [on_device(): pl.pallas_call(functools.partial(kernel, nz, nx, slots, dim), out_shape=j...]
    dot_general x4 -> x0, matrix products: 30.8 us -> none  [advance(): jnp.einsum('slr,lm->rsm', site_piece, env_cols, precision=lax.Precision.H...]
    ppermute x4 -> x0, waiting for transfers between devices: 17.2 us -> none  [shifted(): return lax.ppermute(array, axis, pairs)]
  transfers between devices with their start and end apart: 8 -> 0, of which waited for: 8 -> 0; matrix products, arithmetic and copies ran while one was open for 0% -> 0% of each run, Pallas kernels for 0% -> 0%
where the time goes in v2:
time: 50.7 us
  Pallas kernels  49.5 us (98%)
  local copies, waits for them, and re-layouts  1.19 us (2%)
    pallas_call x1, Pallas kernels, on_device(): pl.pallas_call(functools.partial(kernel, nz, nx, slots, dim), out_shape=j...  49.5 us
    unnamed x1, local copies, waits for them, and re-layouts  1.19 us

profile of v2, /device:TPU:24, one launch (start us, length us, event | category | flops | bytes accessed | tf_op | source)
XLA Modules:
  0.0 50.7 jit_solution(15270623554228989262)
XLA Ops:
  0.0 49.5 %chain.1 = f32[1,32]{1,0:T(1,128)} custom-call(f32[1,2,128,8192]{3,2,1,0:T(8,128)} %sites.1, f32[1,128]{1,0:T(1,128)} %bitcast.4, s32[1,32]{1,0:T(1,128)} %bitcast.5, s32[1,32]{1,0:T(1,128)} %bitcast.6), custom_call_target="tpu_custom_call" | custom-call | tf_op jit(solution)/shard_map/chain/pallas_call | solution.py:354
  49.5 1.2 %copy.6 = f32[32,1]{0,1:T(1,128)} copy(f32[32,1]{0,1:T(1,128)} %bitcast.7) | data formatting | bytes 256

commit v3 on v2

v3 whole, which is shorter than its diff:
```python
import functools

import jax
import jax.numpy as jnp
from jax import lax
from jax.experimental import pallas as pl
from jax.experimental.pallas import tpu as pltpu
from jax.sharding import PartitionSpec as P

EPSILON = 1e-06
LANES = 128
SEGS = 4
MESH = pl.DeviceIdType.MESH
UNMERGED = (8, 3, 1, 0)


def grouping(bonds):
    return (8, 4) if bonds == 64 else (bonds // 2, 1)


def far_first(n):
    return sorted(range(n), key=lambda d: -min(d, n - d))


def unmerged(k, nz):
    return min(UNMERGED[k], nz - 1) if k else nz


def sources(k, nz, nx):
    direct = far_first(nz)[: unmerged(k, nz)]
    listed = [
        (dz, dx, dc) for dz in far_first(nz) for dx in far_first(nx) for dc in ((1, 0) if dz in direct else (0,))
    ]
    if k == SEGS - 1:
        listed.remove((0, 0, 0))
    return listed


def iota(shape, axis):
    return lax.broadcasted_iota(jnp.int32, shape, axis)


def column_of(row, rows):
    shape = (rows, row.shape[1])
    hit = iota(shape, 1) == iota(shape, 0)
    zero = jnp.zeros((), row.dtype)
    return jnp.sum(jnp.where(hit, jnp.broadcast_to(row, shape), zero), axis=1, keepdims=True)


def row_of(column, offset, lanes=LANES):
    shape = (column.shape[0], lanes)
    hit = iota(shape, 1) == iota(shape, 0) + offset
    return jnp.sum(jnp.where(hit, jnp.broadcast_to(column, shape), 0.0), axis=0, keepdims=True)


def total_of(ref, count, rows):
    chains = [ref[i, rows, :] for i in range(min(4, count))]
    for i in range(4, count):
        chains[i % 4] = chains[i % 4] + ref[i, rows, :]
    while len(chains) > 1:
        chains = [sum(chains[i + 1 : i + 2], chains[i]) for i in range(0, len(chains), 2)]
    return chains[0]


def level_offset(k):
    return 2 ** (k + 1) - 2


def kernel(
    nz, nx, slots, dim,
    sites, boundary_hbm, bits_hbm, order_hbm, out,
    tile, split, env0, boundary, bits, order,
    pp1, pp2, pp3, rp1, rp2, rp3,
    pb0, pb1, pb2, pb3, rb0, rb1, rb2, rb3,
    note, notes, fs, fr, s0, r0, s1, r1,
    load_sem, small_sem, notes_sem, rp_sem, note_sem, sp_sem, sb_sem, rb_sem, rb3_sem, f_sem, fr_sem,
    s0_sem, r0_sem, s1_sem, r1_sem,
):
    pp, rp = (None, pp1, pp2, pp3), (None, rp1, rp2, rp3)
    pb, rb = (pb0, pb1, pb2, pb3), (rb0, rb1, rb2, rb3)
    last = SEGS - 1
    bonds, ng = nz * nx * 2, nx * 2
    width = tile.shape[2]
    seg, bond = lax.axis_index("seg"), lax.axis_index("bond")
    z_me, g_me = lax.div(bond, ng), lax.rem(bond, ng)
    x_me, c_me = lax.div(g_me, 2), lax.rem(g_me, 2)
    partner = lax.rem(c_me + 1, 2)
    xs = far_first(nx)
    chips = [(dz, dx) for dz in far_first(nz) for dx in xs]

    def at(dz, dx, core):
        return (lax.rem(z_me + dz, nz) * nx + lax.rem(x_me + dx, nx)) * 2 + core

    def remote(src, dst, send, recv, to_seg, to_bond):
        return pltpu.make_async_remote_copy(
            src_ref=src, dst_ref=dst, send_sem=send, recv_sem=recv,
            device_id={"seg": to_seg, "bond": to_bond}, device_id_type=MESH,
        )

    def wait_bytes(ref, sem):
        pltpu.make_async_copy(ref, ref, sem).wait()

    barrier = pltpu.get_barrier_semaphore()

    def hello(to_seg, to_bond):
        pl.semaphore_signal(barrier, inc=1, device_id={"seg": to_seg, "bond": to_bond}, device_id_type=MESH)

    for k in range(1, SEGS):
        @pl.when(seg == k)
        def _(k=k):
            for dz, dx, dc in sources(k - 1, nz, nx):
                hello(k - 1, at(dz, dx, lax.rem(c_me + dc, 2)))

    everyone = [(dz, dx, dc) for dz, dx in chips for dc in (1, 0) if dz or dx or dc]

    @pl.when(seg == last)
    def _():
        for dz, dx, dc in everyone:
            hello(seg, at(dz, dx, lax.rem(c_me + dc, 2)))
        for k in range(last - 1):
            hello(k, bond)

    @pl.when(seg < last)
    def _():
        hello(last, bond)

    @pl.when(jnp.logical_and(seg > 0, seg < last))
    def _():
        hello(seg, at(0, 0, partner))

    small = [
        pltpu.make_async_copy(src, dst, small_sem.at[i])
        for i, (src, dst) in enumerate(((boundary_hbm, boundary), (bits_hbm, bits), (order_hbm, order)))
    ]
    for copy in small:
        copy.start()

    zs = far_first(nz)

    @pl.loop(0, nz)
    def _(z):
        start = pl.multiple_of(z * ng * width, width)
        pltpu.make_async_copy(sites.at[0, :, :, pl.ds(start, ng * width)], tile.at[z], load_sem.at[z]).start()

    for copy in small:
        copy.wait()
    bits_row = bits[...].astype(jnp.float32)
    order_column = column_of(order[...], slots)

    def bits_at(k):
        parts = [jnp.zeros((1, slots), jnp.float32)] * (LANES // slots)
        parts[k + 1] = bits_row
        return jnp.concatenate(parts, axis=1)

    @pl.when(seg == 0)
    def _():
        env0[...] = jnp.broadcast_to(column_of(boundary[...], width), (width, LANES))

        @pl.loop(0, nz)
        def _(z):
            wait_bytes(tile.at[z], load_sem.at[z])
            for g in range(ng):
                for s in range(2):
                    a = tile[z, s, :, g * width : (g + 1) * width]
                    pb0[z * ng + g, s : s + 1, :] = jnp.sum(a * env0[...], axis=0, keepdims=True)

    @pl.when(seg > 0)
    def _():
        @pl.loop(0, nz)
        def _(z):
            wait_bytes(tile.at[z], load_sem.at[z])
            for s in range(2):
                for g in range(ng):
                    x, core = g // 2, g % 2
                    a = tile[z, s, :, g * width : (g + 1) * width]
                    high = a.astype(jnp.bfloat16)
                    low = (a - high.astype(jnp.float32)).astype(jnp.bfloat16)
                    column = (s * nx + x) * width
                    split[z, core, 0:width, column : column + width] = high
                    split[z, core, width : 2 * width, column : column + width] = low

    for k in range(SEGS):
        @pl.when(seg == k)
        def _(k=k):
            if k == last:
                count = len(everyone) + last
            else:
                count = len(sources(k, nz, nx)) + (1 if k > 0 else 0) + (1 if k < last - 1 else 0)
            pl.semaphore_wait(barrier, count)

    lanes = iota((slots, LANES), 1)

    def pick(where_lane, source):
        return jnp.sum(jnp.where(lanes == where_lane, source, 0.0), axis=1, keepdims=True)

    def site_probability(k, table, bit, node, scale):
        chosen = (bit > 0.5).astype(jnp.int32)
        base = level_offset(k) + node
        m_chosen = pick(base + chosen * 2**k, table) / scale + EPSILON
        m_other = pick(base + (1 - chosen) * 2**k, table) / scale + EPSILON
        return m_chosen / (m_chosen + m_other), node + chosen * 2**k, scale * m_chosen

    def early_sites(known):
        table = jnp.broadcast_to(known, (slots, LANES))
        state = (jnp.zeros((slots, 1), jnp.int32), jnp.full((slots, 1), float(dim), jnp.float32))
        answer = jnp.zeros((slots, 1), jnp.float32)
        for k in range(last):
            bit = pick(order_column + slots * (k + 1), table)
            probability, *state = site_probability(k, table, bit, *state)
            answer = jnp.where(seg == k, probability, answer)
        return answer, state

    def receive(k):
        wait_bytes(rb[k - 1], rb_sem)
        return total_of(rb[k - 1], len(sources(k - 1, nz, nx)), slice(0, 2**k))

    def norm_row(env, k):
        return row_of(jnp.sum(env * env, axis=1, keepdims=True), level_offset(k))

    def report(k, row):
        note[...] = row
        remote(note, notes.at[k], note_sem, notes_sem.at[k], last, bond).start()

    def advance(k):
        rows_in, rows_out = 2**k, 2 ** (k + 1)
        env = receive(k)
        env8 = env
        if rows_in < 8:
            env8 = jnp.concatenate([env, jnp.zeros((8 - rows_in, width), jnp.float32)], axis=0)
        high = env8.astype(jnp.bfloat16).astype(jnp.float32)
        both = jnp.concatenate([high, env8 - high], axis=0).astype(jnp.bfloat16)
        left = jnp.concatenate([both, both], axis=1)
        to_seg, recv = (seg + 1, rb_sem) if k < last else (seg, rb3_sem)
        slot_of = {source: i for i, source in enumerate(sources(k, nz, nx))}

        def blocks(t, core):
            z = lax.rem(z_me + zs[t], nz)
            value = jnp.dot(left, split[z, core], preferred_element_type=jnp.float32)
            value = value[0:8] + value[8:16]
            for x in range(nx):
                for s in range(2):
                    column = (s * nx + x) * width
                    yield x, s * rows_in, value[0:rows_in, column : column + width]

        def to_partner(t, products):
            for x, row, value in products:
                row = x * rows_out + row
                pp[k][t, row : row + rows_in, :] = value
            remote(pp[k].at[t], rp[k].at[t], sp_sem, rp_sem.at[t], seg, at(0, 0, partner)).start()

        def send(t, dc, piece_at):
            for dx in xs:
                source = (zs[t], dx, dc)
                if source in slot_of:
                    x = lax.rem(x_me + dx, nx)
                    to = at(zs[t], dx, lax.rem(c_me + dc, 2))
                    remote(pb[k].at[piece_at + x], rb[k].at[slot_of[source]], sb_sem, recv, to_seg, to).start()

        def own(t, products):
            wait_bytes(rp[k].at[t], rp_sem.at[t])
            for x, row, value in products:
                sent = x * rows_out + row
                pb[k][t * nx + x, row : row + rows_in, :] = value + rp[k][t, sent : sent + rows_in, :]
            send(t, 0, t * nx)

        def direct(dc, t, products):
            piece_at = (t + dc * nz) * nx
            for x, row, value in products:
                pb[k][piece_at + x, row : row + rows_in, :] = value
            send(t, dc, piece_at)

        def norms_ahead(_t, _products):
            share = norm_row(env, k - 1)
            for i in range(last):
                wait_bytes(notes.at[i], notes_sem.at[i])
                share = share + notes[i]
            s0[...] = share
            to_everyone(s0, r0, s0_sem, r0_sem)

        far = unmerged(k, nz)
        both_cores = [(functools.partial(direct, dc), t, (c_me, partner)[dc]) for t in range(far) for dc in (1, 0)]
        exchanged = [(to_partner, t, partner) for t in range(far, nz)]
        steps = both_cores[:2] + exchanged[:2] + both_cores[2:] + exchanged[2:]
        if k == last:
            steps.append((norms_ahead, 0, None))
        steps += [(own, t, c_me) for t in range(far, nz)]
        held = None
        for finish, t, core in steps:
            products = [] if core is None else list(blocks(t, core))
            if held is not None:
                held[0](*held[1:])
            held = (finish, t, products)
        held[0](*held[1:])
        if k < last:
            report(k, norm_row(env, k - 1) + bits_at(k))

    def to_everyone(src, dst, send, recv):
        for i, (dz, dx, dc) in enumerate(everyone):
            remote(src, dst.at[i], send, recv, seg, at(dz, dx, lax.rem(c_me + dc, 2))).start()

    def drain(k):
        if k:
            far = unmerged(k, nz)
            wait_bytes(rp[k].at[pl.ds(far, nz - far)], sp_sem)
        wait_bytes(rb[k], sb_sem)
        if k < last:
            wait_bytes(note, note_sem)

    @pl.when(seg == 0)
    def _():
        for i, (dz, dx, dc) in enumerate(sources(0, nz, nx)):
            to = at(dz, dx, lax.rem(c_me + dc, 2))
            remote(pb0.at[to], rb0.at[i], sb_sem, rb_sem, 1, to).start()
        report(0, bits_at(0))

    for k in range(1, SEGS):
        pl.when(seg == k)(functools.partial(advance, k))

    @pl.when(seg < last)
    def _():
        wait_bytes(fr, fr_sem)
        answer, _state = early_sites(fr[...])
        out[...] = row_of(answer, 0, slots)

    for k in range(last):
        pl.when(seg == k)(functools.partial(drain, k))

    @pl.when(seg == last)
    def _():
        k, rows = last, 2 ** (last + 1)
        wait_bytes(r0, r0_sem)
        share = s0[...]
        known = jnp.where(iota((1, LANES), 1) < slots, share + total_of(r0, bonds - 1, slice(0, 1)), share)
        fs[...] = known
        for to in range(last):
            remote(fs, fr, f_sem, fr_sem, to, bond).start()
        wait_bytes(rb[k], rb3_sem)
        env = pb[k][zs.index(0) * nx + x_me] + total_of(rb[k], len(sources(k, nz, nx)), slice(0, rows))
        s1[...] = norm_row(env, k)
        to_everyone(s1, r1, s1_sem, r1_sem)
        _answer, state = early_sites(known)
        bit = pick(order_column, jnp.concatenate([bits_row] * (LANES // slots), axis=1))
        wait_bytes(r1, r1_sem)
        norms = s1[...] + total_of(r1, bonds - 1, slice(0, 1))
        probability, *_state = site_probability(k, jnp.broadcast_to(norms, (slots, LANES)), bit, *state)
        out[...] = row_of(probability, 0, slots)
        wait_bytes(r0, s0_sem)
        wait_bytes(r1, s1_sem)
        for _i in range(last):
            wait_bytes(fs, f_sem)
        drain(k)


def on_device(nz, nx, sites, boundary, bits, order):
    slots = bits.shape[0]
    width, dim = sites.shape[2], sites.shape[3]
    f32, i32 = jnp.float32, jnp.int32
    bonds, ng = nz * nx * 2, nx * 2
    rows = [2 ** (k + 1) for k in range(SEGS)]
    pieces = [pltpu.VMEM((nz, nx * rows[k], LANES), f32) for k in range(1, SEGS)]
    sends = [pltpu.VMEM(((nz + unmerged(k, nz)) * nx, rows[k], LANES), f32) for k in range(SEGS)]
    receives = [pltpu.VMEM((len(sources(k, nz, nx)), rows[k], LANES), f32) for k in range(SEGS)]
    one = pltpu.VMEM((1, LANES), f32)
    all_rows = pltpu.VMEM((bonds - 1, 1, LANES), f32)
    dma = pltpu.SemaphoreType.DMA
    scratch = [
        pltpu.VMEM((nz, 2, width, ng * width), f32),
        pltpu.VMEM((nz, 2, 2 * width, 2 * nx * width), jnp.bfloat16),
        pltpu.VMEM((width, LANES), f32),
        pltpu.VMEM((1, width), f32), pltpu.VMEM((1, slots), i32), pltpu.VMEM((1, slots), i32),
        *pieces, *pieces, *sends, *receives,
        one, pltpu.VMEM((SEGS - 1, 1, LANES), f32), one, one, one, all_rows, one, all_rows,
        dma((nz,)), dma((3,)), dma((SEGS - 1,)), dma((nz,)), *([dma(())] * 11),
    ]
    hbm = pl.BlockSpec(memory_space=pltpu.HBM)
    answer = pl.pallas_call(
        functools.partial(kernel, nz, nx, slots, dim),
        out_shape=jax.ShapeDtypeStruct((1, slots), f32),
        in_specs=[hbm] * 4,
        out_specs=pl.BlockSpec(memory_space=pltpu.VMEM),
        scratch_shapes=scratch,
        compiler_params=pltpu.CompilerParams(
            collective_id=0, has_side_effects=True, vmem_limit_bytes=67043328
        ),
        name="chain",
    )(sites, boundary.reshape(1, width), bits.T, order.reshape(1, slots))
    return answer.T


def solution(mesh):
    nz, nx = grouping(mesh.shape["bond"])
    return jax.shard_map(
        functools.partial(on_device, nz, nx),
        mesh=mesh,
        in_specs=(P("seg", None, "bond", None), P("bond"), P(None, "seg"), P()),
        out_specs=P(None, "seg"),
        check_vma=False,
    )
```

time: 50.7 us -> 49.6 us (0.978)
  Pallas kernels: 49.5 us -> 48.3 us
    pallas_call x1, Pallas kernels: 49.5 us -> 48.3 us  [on_device(): pl.pallas_call(functools.partial(kernel, nz, nx, slots, dim), out_shape=j...]
where the time goes in v3:
time: 49.6 us; the launch traced here: 49.5 us
  Pallas kernels  48.3 us (97%)
  local copies, waits for them, and re-layouts  1.19 us (2%)
    pallas_call x1, Pallas kernels, on_device(): pl.pallas_call(functools.partial(kernel, nz, nx, slots, dim), out_shape=j...  48.3 us
    unnamed x1, local copies, waits for them, and re-layouts  1.19 us

profile of v3, /device:TPU:24, one launch (start us, length us, event | category | flops | bytes accessed | tf_op | source)
XLA Modules:
  0.0 49.5 jit_solution(11312648929729862296)
XLA Ops:
  0.0 48.3 %chain.1 = f32[1,32]{1,0:T(1,128)} custom-call(f32[1,2,128,8192]{3,2,1,0:T(8,128)} %sites.1, f32[1,128]{1,0:T(1,128)} %bitcast.4, s32[1,32]{1,0:T(1,128)} %bitcast.5, s32[1,32]{1,0:T(1,128)} %bitcast.6), custom_call_target="tpu_custom_call" | custom-call | tf_op jit(solution)/shard_map/chain/pallas_call | solution.py:376
  48.4 1.2 %copy.6 = f32[32,1]{0,1:T(1,128)} copy(f32[32,1]{0,1:T(1,128)} %bitcast.7) | data formatting | bytes 256

commit v4 on v3

--- a/solution.py
+++ b/solution.py
@@ -69,14 +69,14 @@
 def kernel(
     nz, nx, slots, dim,
     sites, boundary_hbm, bits_hbm, order_hbm, out,
-    tile, split, env0, boundary, bits, order,
-    pp1, pp2, pp3, rp1, rp2, rp3,
+    tile, tile2, split, env0, boundary, bits, order,
+    pp1, pp2, rp1, rp2, halves, pe, re,
     pb0, pb1, pb2, pb3, rb0, rb1, rb2, rb3,
     note, notes, fs, fr, s0, r0, s1, r1,
     load_sem, small_sem, notes_sem, rp_sem, note_sem, sp_sem, sb_sem, rb_sem, rb3_sem, f_sem, fr_sem,
-    s0_sem, r0_sem, s1_sem, r1_sem,
+    s0_sem, r0_sem, s1_sem, r1_sem, st_sem, rt_sem, pe_sem, re_sem,
 ):
-    pp, rp = (None, pp1, pp2, pp3), (None, rp1, rp2, rp3)
+    pp, rp = (None, pp1, pp2), (None, rp1, rp2)
     pb, rb = (pb0, pb1, pb2, pb3), (rb0, rb1, rb2, rb3)
     last = SEGS - 1
     bonds, ng = nz * nx * 2, nx * 2
@@ -164,20 +164,21 @@
                     a = tile[z, s, :, g * width : (g + 1) * width]
                     pb0[z * ng + g, s : s + 1, :] = jnp.sum(a * env0[...], axis=0, keepdims=True)
 
-    @pl.when(seg > 0)
+    def split_into(z, half, s, x, a):
+        high = a.astype(jnp.bfloat16)
+        low = (a - high.astype(jnp.float32)).astype(jnp.bfloat16)
+        column = (s * nx + x) * width
+        split[z, half, 0:width, column : column + width] = high
+        split[z, half, width : 2 * width, column : column + width] = low
+
+    @pl.when(jnp.logical_and(seg > 0, seg < last))
     def _():
         @pl.loop(0, nz)
         def _(z):
             wait_bytes(tile.at[z], load_sem.at[z])
             for s in range(2):
                 for g in range(ng):
-                    x, core = g // 2, g % 2
-                    a = tile[z, s, :, g * width : (g + 1) * width]
-                    high = a.astype(jnp.bfloat16)
-                    low = (a - high.astype(jnp.float32)).astype(jnp.bfloat16)
-                    column = (s * nx + x) * width
-                    split[z, core, 0:width, column : column + width] = high
-                    split[z, core, width : 2 * width, column : column + width] = low
+                    split_into(z, g % 2, s, g // 2, tile[z, s, :, g * width : (g + 1) * width])
 
     for k in range(SEGS):
         @pl.when(seg == k)
@@ -187,6 +188,32 @@
             else:
                 count = len(sources(k, nz, nx)) + (1 if k > 0 else 0) + (1 if k < last - 1 else 0)
             pl.semaphore_wait(barrier, count)
+
+    @pl.when(seg == last)
+    def _():
+        @pl.loop(0, nz)
+        def _(z):
+            wait_bytes(tile.at[z], load_sem.at[z])
+            for x in range(nx):
+                start = pl.multiple_of((x * 2 + partner) * width, width)
+                remote(
+                    tile.at[z, :, :, pl.ds(start, width)], tile2.at[z, :, :, pl.ds(x * width, width)],
+                    st_sem.at[z], rt_sem.at[z], seg, at(0, 0, partner),
+                ).start()
+
+        @pl.loop(0, nz)
+        def _(z):
+            for s in range(2):
+                for x in range(nx):
+                    start = pl.multiple_of((x * 2 + c_me) * width, width)
+                    split_into(z, 0, s, x, tile[z, s, :, pl.ds(start, width)])
+
+        @pl.loop(0, nz)
+        def _(z):
+            wait_bytes(tile2.at[z], rt_sem.at[z])
+            for s in range(2):
+                for x in range(nx):
+                    split_into(z, 1, s, x, tile2[z, s, :, x * width : (x + 1) * width])
 
     lanes = iota((slots, LANES), 1)
 
@@ -221,16 +248,63 @@
         note[...] = row
         remote(note, notes.at[k], note_sem, notes_sem.at[k], last, bond).start()
 
+    def left_of(env):
+        rows = env.shape[0]
+        if rows < 8:
+            env = jnp.concatenate([env, jnp.zeros((8 - rows, width), jnp.float32)], axis=0)
+        high = env.astype(jnp.bfloat16).astype(jnp.float32)
+        both = jnp.concatenate([high, env - high], axis=0).astype(jnp.bfloat16)
+        return jnp.concatenate([both, both], axis=1)
+
+    def advance_last():
+        k, rows_in = last, 2**last
+        env = receive(k)
+        pe[...] = env
+        remote(pe, re, pe_sem, re_sem, seg, at(0, 0, partner)).start()
+        slot_of = {source: i for i, source in enumerate(sources(k, nz, nx))}
+
+        def half(left, t, which):
+            z = lax.rem(z_me + zs[t], nz)
+            value = jnp.dot(left, split[z, which], preferred_element_type=jnp.float32)
+            return value[0:8] + value[8:16]
+
+        left = left_of(env)
+        share = norm_row(env, k - 1)
+        for i in range(last):
+            wait_bytes(notes.at[i], notes_sem.at[i])
+            share = share + notes[i]
+        s0[...] = share
+        each = -(-len(everyone) // nz)
+        for t in range(nz):
+            halves[t] = half(left, t, 0)
+            to_everyone(s0, r0, s0_sem, r0_sem, t * each, (t + 1) * each)
+        wait_bytes(re, re_sem)
+        left = left_of(re[...])
+
+        def finish(t, value):
+            value = value + halves[t]
+            for x in range(nx):
+                for s in range(2):
+                    column = (s * nx + x) * width
+                    pb[k][t * nx + x, s * rows_in : (s + 1) * rows_in, :] = value[:, column : column + width]
+            for dx in xs:
+                source = (zs[t], dx, 0)
+                if source in slot_of:
+                    x = lax.rem(x_me + dx, nx)
+                    remote(
+                        pb[k].at[t * nx + x], rb[k].at[slot_of[source]], sb_sem, rb3_sem, seg, at(zs[t], dx, c_me)
+                    ).start()
+
+        held = half(left, 0, 1)
+        for t in range(1, nz):
+            value = half(left, t, 1)
+            finish(t - 1, held)
+            held = value
+        finish(nz - 1, held)
     def advance(k):
         rows_in, rows_out = 2**k, 2 ** (k + 1)
         env = receive(k)
-        env8 = env
-        if rows_in < 8:
-            env8 = jnp.concatenate([env, jnp.zeros((8 - rows_in, width), jnp.float32)], axis=0)
-        high = env8.astype(jnp.bfloat16).astype(jnp.float32)
-        both = jnp.concatenate([high, env8 - high], axis=0).astype(jnp.bfloat16)
-        left = jnp.concatenate([both, both], axis=1)
-        to_seg, recv = (seg + 1, rb_sem) if k < last else (seg, rb3_sem)
+        left = left_of(env)
         slot_of = {source: i for i, source in enumerate(sources(k, nz, nx))}
 
         def blocks(t, core):
@@ -254,7 +328,7 @@
                 if source in slot_of:
                     x = lax.rem(x_me + dx, nx)
                     to = at(zs[t], dx, lax.rem(c_me + dc, 2))
-                    remote(pb[k].at[piece_at + x], rb[k].at[slot_of[source]], sb_sem, recv, to_seg, to).start()
+                    remote(pb[k].at[piece_at + x], rb[k].at[slot_of[source]], sb_sem, rb_sem, seg + 1, to).start()
 
         def own(t, products):
             wait_bytes(rp[k].at[t], rp_sem.at[t])
@@ -269,37 +343,30 @@
                 pb[k][piece_at + x, row : row + rows_in, :] = value
             send(t, dc, piece_at)
 
-        def norms_ahead(_t, _products):
-            share = norm_row(env, k - 1)
-            for i in range(last):
-                wait_bytes(notes.at[i], notes_sem.at[i])
-                share = share + notes[i]
-            s0[...] = share
-            to_everyone(s0, r0, s0_sem, r0_sem)
-
         far = unmerged(k, nz)
         both_cores = [(functools.partial(direct, dc), t, (c_me, partner)[dc]) for t in range(far) for dc in (1, 0)]
         exchanged = [(to_partner, t, partner) for t in range(far, nz)]
         steps = both_cores[:2] + exchanged[:2] + both_cores[2:] + exchanged[2:]
-        if k == last:
-            steps.append((norms_ahead, 0, None))
         steps += [(own, t, c_me) for t in range(far, nz)]
         held = None
         for finish, t, core in steps:
-            products = [] if core is None else list(blocks(t, core))
+            products = list(blocks(t, core))
             if held is not None:
                 held[0](*held[1:])
             held = (finish, t, products)
         held[0](*held[1:])
-        if k < last:
-            report(k, norm_row(env, k - 1) + bits_at(k))
-
-    def to_everyone(src, dst, send, recv):
-        for i, (dz, dx, dc) in enumerate(everyone):
+        report(k, norm_row(env, k - 1) + bits_at(k))
+
+    def to_everyone(src, dst, send, recv, start=0, stop=None):
+        for i, (dz, dx, dc) in list(enumerate(everyone))[start:stop]:
             remote(src, dst.at[i], send, recv, seg, at(dz, dx, lax.rem(c_me + dc, 2))).start()
 
     def drain(k):
-        if k:
+        if k == last:
+            wait_bytes(pe, pe_sem)
+            for z in range(nz):
+                wait_bytes(tile2.at[z], st_sem.at[z])
+        elif k:
             far = unmerged(k, nz)
             wait_bytes(rp[k].at[pl.ds(far, nz - far)], sp_sem)
         wait_bytes(rb[k], sb_sem)
@@ -313,8 +380,9 @@
             remote(pb0.at[to], rb0.at[i], sb_sem, rb_sem, 1, to).start()
         report(0, bits_at(0))
 
-    for k in range(1, SEGS):
+    for k in range(1, last):
         pl.when(seg == k)(functools.partial(advance, k))
+    pl.when(seg == last)(advance_last)
 
     @pl.when(seg < last)
     def _():
@@ -357,7 +425,7 @@
     f32, i32 = jnp.float32, jnp.int32
     bonds, ng = nz * nx * 2, nx * 2
     rows = [2 ** (k + 1) for k in range(SEGS)]
-    pieces = [pltpu.VMEM((nz, nx * rows[k], LANES), f32) for k in range(1, SEGS)]
+    pieces = [pltpu.VMEM((nz, nx * rows[k], LANES), f32) for k in range(1, SEGS - 1)]
     sends = [pltpu.VMEM(((nz + unmerged(k, nz)) * nx, rows[k], LANES), f32) for k in range(SEGS)]
     receives = [pltpu.VMEM((len(sources(k, nz, nx)), rows[k], LANES), f32) for k in range(SEGS)]
     one = pltpu.VMEM((1, LANES), f32)
@@ -365,12 +433,14 @@
     dma = pltpu.SemaphoreType.DMA
     scratch = [
         pltpu.VMEM((nz, 2, width, ng * width), f32),
+        pltpu.VMEM((nz, 2, width, nx * width), f32),
         pltpu.VMEM((nz, 2, 2 * width, 2 * nx * width), jnp.bfloat16),
         pltpu.VMEM((width, LANES), f32),
         pltpu.VMEM((1, width), f32), pltpu.VMEM((1, slots), i32), pltpu.VMEM((1, slots), i32),
-        *pieces, *pieces, *sends, *receives,
+        *pieces, *pieces, pltpu.VMEM((nz, 8, 2 * nx * width), f32), pltpu.VMEM((8, LANES), f32), pltpu.VMEM((8, LANES), f32),
+        *sends, *receives,
         one, pltpu.VMEM((SEGS - 1, 1, LANES), f32), one, one, one, all_rows, one, all_rows,
-        dma((nz,)), dma((3,)), dma((SEGS - 1,)), dma((nz,)), *([dma(())] * 11),
+        dma((nz,)), dma((3,)), dma((SEGS - 1,)), dma((nz,)), *([dma(())] * 11), dma((nz,)), dma((nz,)), dma(()), dma(()),
     ]
     hbm = pl.BlockSpec(memory_space=pltpu.HBM)
     answer = pl.pallas_call(

time: 49.6 us -> 49.2 us (level)
  no operation moved by 1% of the time
where the time goes in v4:
time: 49.2 us; the launch traced here: 49.1 us
  Pallas kernels  47.9 us (97%)
  local copies, waits for them, and re-layouts  1.19 us (2%)
    pallas_call x1, Pallas kernels, on_device(): pl.pallas_call(functools.partial(kernel, nz, nx, slots, dim), out_shape=j...  47.9 us
    unnamed x1, local copies, waits for them, and re-layouts  1.19 us

profile of v4, /device:TPU:24, one launch (start us, length us, event | category | flops | bytes accessed | tf_op | source)
XLA Modules:
  0.0 49.1 jit_solution(1150398363679845290)
XLA Ops:
  0.0 47.9 %chain.1 = f32[1,32]{1,0:T(1,128)} custom-call(f32[1,2,128,8192]{3,2,1,0:T(8,128)} %sites.1, f32[1,128]{1,0:T(1,128)} %bitcast.4, s32[1,32]{1,0:T(1,128)} %bitcast.5, s32[1,32]{1,0:T(1,128)} %bitcast.6), custom_call_target="tpu_custom_call" | custom-call | tf_op jit(solution)/shard_map/chain/pallas_call | solution.py:446
  48.0 1.2 %copy.6 = f32[32,1]{0,1:T(1,128)} copy(f32[32,1]{0,1:T(1,128)} %bitcast.7) | data formatting | bytes 256

commit v5 on v4

--- a/solution.py
+++ b/solution.py
@@ -346,7 +346,7 @@
         far = unmerged(k, nz)
         both_cores = [(functools.partial(direct, dc), t, (c_me, partner)[dc]) for t in range(far) for dc in (1, 0)]
         exchanged = [(to_partner, t, partner) for t in range(far, nz)]
-        steps = both_cores[:2] + exchanged[:2] + both_cores[2:] + exchanged[2:]
+        steps = exchanged[:2] + both_cores + exchanged[2:]
         steps += [(own, t, c_me) for t in range(far, nz)]
         held = None
         for finish, t, core in steps:

time: 49.2 us -> 49.4 us (level)
  no operation moved by 1% of the time
where the time goes in v5:
time: 49.4 us; the launch traced here: 49.3 us
  Pallas kernels  48.1 us (97%)
  local copies, waits for them, and re-layouts  1.19 us (2%)
    pallas_call x1, Pallas kernels, on_device(): pl.pallas_call(functools.partial(kernel, nz, nx, slots, dim), out_shape=j...  48.1 us
    unnamed x1, local copies, waits for them, and re-layouts  1.19 us

profile of v5, /device:TPU:24, one launch (start us, length us, event | category | flops | bytes accessed | tf_op | source)
XLA Modules:
  0.0 49.3 jit_solution(13460631755278029794)
XLA Ops:
  0.0 48.1 %chain.1 = f32[1,32]{1,0:T(1,128)} custom-call(f32[1,2,128,8192]{3,2,1,0:T(8,128)} %sites.1, f32[1,128]{1,0:T(1,128)} %bitcast.4, s32[1,32]{1,0:T(1,128)} %bitcast.5, s32[1,32]{1,0:T(1,128)} %bitcast.6), custom_call_target="tpu_custom_call" | custom-call | tf_op jit(solution)/shard_map/chain/pallas_call | solution.py:446
  48.1 1.2 %copy.6 = f32[32,1]{0,1:T(1,128)} copy(f32[32,1]{0,1:T(1,128)} %bitcast.7) | data formatting | bytes 256
